TPU v7x, 128 devices: a whole 4x4x4 slice. The times are simulated.
128 devices in a mesh: dp: 8 (over x, core), seq: 16 (over z, y).
Axes of the slice: x: 4, y: 4, z: 4, core: 2. Of those that a mesh axis runs over, the one named last changes fastest.
Arguments:
- tokens: bfloat16 [8, 12288, 2560], P('dp', 'seq'), may hold values from -6 to 6
- w_xbc: bfloat16 [2560, 2816], P(('dp', 'seq')), may hold values from -0.125 to 0.125
- conv_weight: float32 [4, 2816], replicated, may hold values from -3 to 3
- conv_bias: float32 [2816], replicated, may hold values from -2 to 2
- a_log: float32 [40], replicated, may hold values from -13 to -3
- dt_in: float32 [8, 40, 12288], P('dp', None, 'seq'), may hold values from -2 to 98304
- d_skip: float32 [40], replicated, may hold values from 0.5 to 1.5
- norm_gain: float32 [2560], replicated, may hold values from 0.25 to 1.75
Outputs:
- normed: bfloat16 [8, 12288, 2560], P('dp', 'seq')
All inputs are finite; a program needn't handle non-finite values.
Results may differ from a plain program's by a relative error of at most 0.012.
Values may be sent and summed in bfloat16 or wider, within the bound.
A program may use at most 128 MiB of HBM per device.

v0:
```python
import jax
import jax.numpy as jnp
from jax import lax
from jax.sharding import PartitionSpec as P

GROUP = 256


def passed_along(value, axis, by):
    length = lax.axis_size(axis)
    pairs = [(i, i + by) for i in range(length) if 0 <= i + by < length]
    return lax.ppermute(value, axis, pairs)


def prefix(value, axis, join, neutral):
    count, mine = (lax.axis_size(axis), lax.axis_index(axis))
    pieces = jax.tree.map(lambda part: lax.all_gather(part, axis), value)
    running = jax.tree.map(
        lambda part, zero: jnp.full_like(part, 0) + jnp.asarray(zero, part.dtype), value, neutral
    )

    def hop(position, running):
        longer = join(running, jax.tree.map(lambda part: part[position], pieces))
        return jax.tree.map(lambda new, old: jnp.where(position < mine, new, old), longer, running)

    return lax.fori_loop(0, count - 1, hop, running)


def block_state(x_block, b_block, dt_block, decay_block):
    heads = dt_block.shape[0]
    length = dt_block.shape[1]
    x_heads = x_block.astype(jnp.float32).reshape(length, heads, -1)
    cumul = jnp.cumsum(decay_block, axis=1)
    tail_weight = jnp.exp(cumul[:, -1:] - cumul) * dt_block
    weighted = tail_weight.T[:, :, None] * x_heads
    span_state = jnp.einsum(
        "jhp,jn->hpn", weighted, b_block.astype(jnp.float32), precision=lax.Precision.HIGH
    )
    return (span_state, cumul[:, -1])


def block_inner(x_block, b_block, c_block, dt_block, decay_block):
    heads = dt_block.shape[0]
    length = dt_block.shape[1]
    x_heads = x_block.astype(jnp.float32).reshape(length, heads, -1)
    cumul = jnp.cumsum(decay_block, axis=1)
    spread = cumul[:, :, None] - cumul[:, None, :]
    lower = jnp.arange(length)[:, None] >= jnp.arange(length)[None, :]
    decay_mat = jnp.exp(jnp.where(lower[None], spread, -jnp.inf))
    scores = jnp.dot(c_block, b_block.T, preferred_element_type=jnp.float32)
    mixing = decay_mat * scores[None] * dt_block[:, None, :]
    y_inner = jnp.einsum("hij,jhp->ihp", mixing, x_heads, precision=lax.Precision.HIGH)
    return (y_inner, cumul, x_heads)


def combine_carry(earlier, later):
    return (earlier[0] + later[0], jnp.exp(later[0])[:, None, None] * earlier[1] + later[1])


def local(tokens, w_xbc, conv_weight, conv_bias, a_log, dt_in, d_skip, norm_gain):
    token_rows = tokens[0]
    tok_count = token_rows.shape[0]
    heads = a_log.shape[0]
    width_x = norm_gain.shape[0]
    head_size = width_x // heads
    channels = w_xbc.shape[1]
    state_size = (channels - width_x) // 2
    kernel = conv_weight.shape[0]
    projected = jnp.dot(
        token_rows,
        lax.all_gather(w_xbc, ("dp", "seq"), axis=0, tiled=True),
        preferred_element_type=jnp.float32,
    )
    xbc = projected.astype(jnp.bfloat16)
    rim_rows = passed_along(xbc[tok_count - (kernel - 1) :], "seq", 1)
    padded = jnp.concatenate([rim_rows, xbc], axis=0)
    accum = conv_bias[None, :] + jnp.zeros((tok_count, channels), jnp.float32)
    for tap_index in range(kernel):
        accum = accum + conv_weight[tap_index][None, :] * padded[
            tap_index : tap_index + tok_count
        ].astype(jnp.float32)
    conv_out = jax.nn.silu(accum).astype(jnp.bfloat16)
    step_size = jax.nn.softplus(dt_in[0])
    log_decay = -jnp.exp(a_log)[:, None] * step_size
    blocks = tok_count // GROUP
    gain_heads = norm_gain.reshape(heads, head_size)[None]
    pieces = []
    own_state = jnp.zeros((heads, head_size, state_size), jnp.float32)
    own_decay = jnp.zeros((heads,), jnp.float32)
    for block_index in range(blocks):
        lo_row = block_index * GROUP
        block_rows = conv_out[lo_row : lo_row + GROUP]
        x_block = block_rows[:, :width_x]
        b_block = block_rows[:, width_x : width_x + state_size]
        c_block = block_rows[:, width_x + state_size :]
        dt_block = step_size[:, lo_row : lo_row + GROUP]
        decay_block = log_decay[:, lo_row : lo_row + GROUP]
        span_state, totals = block_state(x_block, b_block, dt_block, decay_block)
        own_state = jnp.exp(totals)[:, None, None] * own_state + span_state
        own_decay = own_decay + totals
        pieces.append((x_block, b_block, c_block, dt_block, decay_block, span_state, totals))
    identity = (jnp.zeros_like(own_decay), jnp.zeros_like(own_state))
    earlier_decay, incoming = prefix((own_decay, own_state), "seq", combine_carry, identity)
    state = incoming
    outputs = []
    for block_index in range(blocks):
        x_block, b_block, c_block, dt_block, decay_block, span_state, totals = pieces[block_index]
        y_inner, cumul, x_heads = block_inner(x_block, b_block, c_block, dt_block, decay_block)
        from_state = jnp.einsum(
            "in,hpn->ihp", c_block.astype(jnp.float32), state, precision=lax.Precision.HIGH
        )
        ssd = y_inner + jnp.exp(cumul).T[:, :, None] * from_state + d_skip[None, :, None] * x_heads
        mean_sq = jnp.mean(ssd * ssd, axis=-1, keepdims=True)
        scaled = ssd * lax.rsqrt(mean_sq + 1e-05) * gain_heads
        outputs.append(scaled.reshape(GROUP, width_x).astype(jnp.bfloat16))
        state = jnp.exp(totals)[:, None, None] * state + span_state
    return jnp.concatenate(outputs, axis=0)[None]


def solution(mesh):
    return jax.shard_map(
        local,
        mesh=mesh,
        in_specs=(
            P("dp", "seq", None),
            P(("dp", "seq"), None),
            P(),
            P(),
            P(),
            P("dp", None, "seq"),
            P(),
            P(),
        ),
        out_specs=P("dp", "seq", None),
        check_vma=False,
    )
```

profile of v0, /device:TPU:1, one launch (start us, length us, event | category | flops | bytes accessed | tf_op | source)
XLA Modules:
  0.0 367.9 jit_solution(12167026714870173154)
XLA Ops:
  6.5 0.7 all-gather.8.cloned.1.call-update
  8.0 1.0 compare_select_fusion
  12.4 0.8 fusion.91
  13.2 81.4 %all-gather.8.cloned.1.call-done = bf16[128,20,2816]{2,1,0:T(8,128)(2,1)} async-done(((bf16[1,20,2816]{2,1,0:T(8,128)(2,1)}), bf16[128,20,2816]{2,1,0:T(8,128)(2,1)}) %all-gather.8.cloned.1.call-update) | async-done | bytes 14417936 | tf_op jit(solution)/shard_map/all_gather | solution.py:71
  94.6 20.5 %reshape.252 = bf16[2560,2816]{1,0:T(8,128)(2,1)} reshape(bf16[128,20,2816]{2,1,0:T(8,128)(2,1)} %all-gather.8.cloned.1.call-done) | data formatting | bytes 28835840
  115.1 16.4 %convolution_convert_fusion = bf16[768,2816]{1,0:T(8,128)(2,1)S(1)} fusion(bf16[2560,2816]{1,0:T(8,128)(2,1)} %reshape.252, bf16[1,768,2560]{2,1,0:T(8,128)(2,1)} %param.10), kind=kOutput, calls=%fused_computation.42 | convolution fusion | flops 11075125248 | bytes 22675456 | tf_op jit(solution)/shard_map/dot_general | solution.py:69
  131.6 3.1 collective-permute-start
  134.9 0.7 collective-permute-done
  135.6 6.3 %multiply_convert_fusion = bf16[768,2816]{1,0:T(8,128)(2,1)S(1)} fusion(bf16[768,2816]{1,0:T(8,128)(2,1)S(1)} %convolution_convert_fusion, bf16[3,2816]{1,0:T(4,128)(2,1)S(1)} %collective-permute-done, f32[2816]{0:T(1024)S(1)} %get-tuple-element.120, f32[2816]{0:T(1024)S(1)} %get-tuple-element.121, f32[2816]{0:T(1024)S(1)} %get-tuple-element.119, ...), kind=kLoop, calls=%fused_computation.21 | loop fusion | flops 56229888 | bytes 8723968 | tf_op jit(solution)/shard_map/convert_element_type | solution.py:82
  141.9 2.0 fusion.90
  143.9 0.8 copy-done
  144.8 1.6 copy.33
  146.4 2.9 copy.40
  149.3 1.5 copy.41
  150.8 1.8 fusion.40
  152.6 1.7 fusion.42
  154.4 1.0 copy-done.1
  155.4 2.9 fusion.52
  159.8 34.8 %all-reduce = f32[640]{0:T(1024)S(1)} all-reduce(f32[640]{0:T(1024)S(1)} %dynamic-update-slice), channel_id=2, replica_groups=mesh['dp'=8,'seq'=16] {'seq'}, use_global_device_ids=true, to_apply=%add | all-reduce | flops 640 | bytes 5120
  195.9 1.1 fusion.73
  197.0 1.1 fusion.76
  198.0 1.1 fusion.83
  199.1 93.6 %all-gather.6.cloned.1.call-done = f32[640,64,128]{2,1,0:T(8,128)} async-done(((f32[40,64,128]{2,1,0:T(8,128)}), f32[640,64,128]{2,1,0:T(8,128)}) %all-gather.6.cloned.1.call-update) | async-done | bytes 20971536 | tf_op jit(solution)/shard_map/all_gather | solution.py:17
  292.7 35.1 %while.14 = (s32[]{:T(128)}, f32[40,64,128]{2,1,0:T(8,128)S(1)}, s32[]{:T(128)}, f32[16,40]{1,0:T(8,128)}, f32[16,40,64,128]{3,2,1,0:T(8,128)}, /*index=5*/s32[]{:T(128)}, s32[]{:T(128)}) while((s32[]{:T(128)}, f32[40,64,128]{2,1,0:T(8,128)S(1)}, s32[]{:T(128)}, f32[16,40]{1,0:T(8,128)}, f32[16,40,64,128]{3,2,1,0:T(8,128)}, ...), condition=%wide.region_7.8_spmd.clone, body=%wide.region_6.7_spmd.clone.sunk | while | flops 1310724 | bytes 3932745 | solution.py:26
  293.4 1.6 fusion.99
  295.0 0.7 exponential_bitcast_fusion.5
  295.7 1.6 fusion.99
  297.4 0.7 exponential_bitcast_fusion.5
  298.0 1.6 fusion.99
  299.7 0.7 exponential_bitcast_fusion.5
  300.4 1.6 fusion.99
  302.0 0.7 exponential_bitcast_fusion.5
  302.7 1.6 fusion.99
  304.3 0.7 exponential_bitcast_fusion.5
  305.0 1.6 fusion.99
  306.7 0.7 exponential_bitcast_fusion.5
  307.4 1.6 fusion.99
  309.0 0.7 exponential_bitcast_fusion.5
  309.7 1.6 fusion.99
  311.3 0.7 exponential_bitcast_fusion.5
  312.0 1.6 fusion.99
  313.6 0.7 exponential_bitcast_fusion.5
  314.3 1.6 fusion.99
  316.0 0.7 exponential_bitcast_fusion.5
  316.7 1.6 fusion.99
  318.3 0.7 exponential_bitcast_fusion.5
  319.0 1.6 fusion.99
  320.6 0.7 exponential_bitcast_fusion.5
  321.3 1.6 fusion.99
  323.0 0.7 exponential_bitcast_fusion.5
  323.7 1.6 fusion.99
  325.3 0.7 exponential_bitcast_fusion.5
  326.0 1.6 fusion.99
  327.8 2.2 fusion.53
  330.0 1.7 fusion.60
  331.8 1.8 fusion.70
  333.7 5.3 %multiply_reduce_fusion = (f32[256,40]{0,1:T(8,128)S(1)}, f32[256,40,64]{0,2,1:T(8,128)S(1)}) fusion(bf16[256,40,64]{0,2,1:T(8,128)(2,1)S(1)} %bitcast.140, f32[40]{0:T(128)S(1)} %copy-done.21, f32[256,40,64]{0,2,1:T(8,128)S(1)} %fusion.53, f32[256,40]{0,1:T(8,128)S(1)} %copy-done.16, f32[40,256]{1,0:T(8,128)S(1)} %copy-done.15, ...), kind=kOutput, calls=%fused_computation.64 | convolution fusion | flops 1021696000 | bytes 7045280 | tf_op jit(solution)/shard_map/hij,jhp->ihp/dot_general | solution.py:52
  339.1 5.5 %multiply_reduce_fusion.1 = (f32[256,40]{0,1:T(8,128)S(1)}, f32[256,40,64]{0,2,1:T(8,128)S(1)}) fusion(bf16[256,40,64]{0,2,1:T(8,128)(2,1)S(1)} %bitcast.138, f32[40]{0:T(128)S(1)} %copy-done.21, f32[256,40,64]{0,2,1:T(8,128)S(1)} %fusion.60, f32[256,40]{0,1:T(8,128)S(1)} %copy-done.14, f32[40,256]{1,0:T(8,128)S(1)} %copy-done.13, ...), kind=kOutput, calls=%fused_computation.66 | convolution fusion | flops 1021696000 | bytes 7045280 | tf_op jit(solution)/shard_map/hij,jhp->ihp/dot_general | solution.py:52
  344.6 5.2 %multiply_reduce_fusion.2 = (f32[256,40]{0,1:T(8,128)S(1)}, f32[256,40,64]{0,2,1:T(8,128)S(1)}) fusion(bf16[256,40,64]{0,2,1:T(8,128)(2,1)S(1)} %bitcast.136, f32[40]{0:T(128)S(1)} %copy-done.21, f32[256,40,64]{0,2,1:T(8,128)S(1)} %fusion.70, f32[256,40]{0,1:T(8,128)S(1)} %copy-done.12, f32[40,256]{1,0:T(8,128)S(1)} %copy-done.11, ...), kind=kOutput, calls=%fused_computation.68 | convolution fusion | flops 1021696000 | bytes 7045280 | tf_op jit(solution)/shard_map/hij,jhp->ihp/dot_general | solution.py:52
  349.9 2.2 multiply_convert_fusion.3
  352.1 2.4 copy.42
  354.6 1.6 copy.43
  356.1 1.6 copy.44
  357.7 3.3 maximum_bitcast_fusion
  (83 shorter events, 7.3 us)
Async XLA Ops:
  6.5 88.1 %all-gather.8.cloned.1.call-start = ((), (), s32[]{:S(2)}) async-start(), calls=%async_computation.1 | async-start | bytes 17436672 | tf_op jit(solution)/shard_map/all_gather | solution.py:71
  7.3 285.4 %all-gather.6.cloned.1.call-start = ((), (), s32[]{:S(2)}) async-start(), calls=%async_computation | async-start | bytes 22282240 | tf_op jit(solution)/shard_map/all_gather | solution.py:17
  115.1 19.6 %copy-start.10 = (f32[4,2816]{1,0:T(4,128)S(1)}, f32[4,2816]{1,0:T(4,128)}, u32[]{:S(2)}) copy-start(f32[4,2816]{1,0:T(4,128)} %param.12) | copy-start | bytes 135172
  115.1 20.5 %copy-start.17 = (f32[2816]{0:T(1024)S(1)}, f32[2816]{0:T(1024)}, u32[]{:S(2)}) copy-start(f32[2816]{0:T(1024)} %param.13) | copy-start | bytes 33796
  131.6 4.0 %collective-permute-start = (bf16[3,2816]{1,0:T(4,128)(2,1)S(1)}, bf16[3,2816]{1,0:T(4,128)(2,1)S(1)}, u32[]{:S(2)}, u32[]{:S(2)}) collective-permute-start(bf16[3,2816]{1,0:T(4,128)(2,1)S(1)} %slice.143), channel_id=1, source_target_pairs={{0,1},{1,2},{2,3},{3,4},{4,5},{5,6},{6,7},{7,8},{8,9},{9,10},{10,1... | collective-permute-start | bytes 50696 | tf_op jit(solution)/shard_map/ppermute | solution.py:12
  134.8 19.5 %copy-start.20 = (f32[40]{0:T(128)}, f32[40]{0:T(128)S(1)}, u32[]{:S(2)}) copy-start(f32[40]{0:T(128)S(1)} %exp.81) | copy-start | bytes 484
  141.9 2.8 copy-start
  146.4 4.4 %copy-start.2 = (bf16[256,2560]{0,1:T(8,128)(2,1)}, bf16[256,2560]{0,1:T(8,128)(2,1)S(1)}, u32[]{:S(2)}) copy-start(bf16[256,2560]{0,1:T(8,128)(2,1)S(1)} %copy.33) | copy-start | bytes 3932164
  150.8 1.9 copy-start.4
  150.8 4.6 %copy-start.6 = (bf16[256,2560]{0,1:T(8,128)(2,1)S(1)}, bf16[256,2560]{0,1:T(8,128)(2,1)}, u32[]{:S(2)}) copy-start(bf16[256,2560]{0,1:T(8,128)(2,1)} %copy.41) | copy-start | bytes 3932164
  154.3 1.0 copy-start.1
  155.4 2.9 copy-start.22
  155.4 39.8 %copy-start.18 = (f32[2560]{0:T(1024)S(1)}, f32[2560]{0:T(1024)}, u32[]{:S(2)}) copy-start(f32[2560]{0:T(1024)} %param.17) | copy-start | bytes 30724
  327.8 2.2 copy-start.19
  331.8 1.8 copy-start.7
  331.8 1.8 copy-start.9
  331.8 1.8 copy-start.15
  331.8 1.8 copy-start.16
  331.8 1.8 copy-start.21
  333.7 5.3 %copy-start.5 = (bf16[256,2560]{0,1:T(8,128)(2,1)S(1)}, bf16[256,2560]{0,1:T(8,128)(2,1)}, u32[]{:S(2)}) copy-start(bf16[256,2560]{0,1:T(8,128)(2,1)} %copy.40) | copy-start | bytes 3932164
  333.7 5.3 %copy-start.13 = (f32[40,256]{1,0:T(8,128)S(1)}, f32[40,256]{1,0:T(8,128)}, u32[]{:S(2)}) copy-start(f32[40,256]{1,0:T(8,128)} %get-tuple-element.143) | copy-start | bytes 122884
  333.7 5.3 %copy-start.14 = (f32[256,40]{0,1:T(8,128)S(1)}, f32[256,40]{0,1:T(8,128)}, u32[]{:S(2)}) copy-start(f32[256,40]{0,1:T(8,128)} %get-tuple-element.152) | copy-start | bytes 122884
  339.0 5.6 %copy-start.3 = (bf16[256,2560]{0,1:T(8,128)(2,1)S(1)}, bf16[256,2560]{0,1:T(8,128)(2,1)}, u32[]{:S(2)}) copy-start(bf16[256,2560]{0,1:T(8,128)(2,1)} %copy-done.2) | copy-start | bytes 3932164
  339.0 5.6 %copy-start.11 = (f32[40,256]{1,0:T(8,128)S(1)}, f32[40,256]{1,0:T(8,128)}, u32[]{:S(2)}) copy-start(f32[40,256]{1,0:T(8,128)} %get-tuple-element.139) | copy-start | bytes 122884
  339.0 5.6 %copy-start.12 = (f32[256,40]{0,1:T(8,128)S(1)}, f32[256,40]{0,1:T(8,128)}, u32[]{:S(2)}) copy-start(f32[256,40]{0,1:T(8,128)} %get-tuple-element.150) | copy-start | bytes 122884
  356.1 1.6 copy-start.8
Sparse Core Ops, SparseCore 0:
  10.4 84.2 all-gather.7
  158.4 134.2 all-gather.5
where the time goes:
time: 370 us; the launch traced here: 368 us
  waiting for transfers between devices  177 us (48%)
  local copies, waits for them, and re-layouts  48.7 us (13%)
  matrix products  47.7 us (13%)
  other arithmetic  42.2 us (11%)
  blocking collectives  34.8 us (9%)
  between operations  14.5 us (4%)
    all_gather x1, waiting for transfers between devices, prefix(): pieces = jax.tree.map(lambda part: lax.all_gather(part, axis), value)  93.6 us
    all_gather x1, waiting for transfers between devices, local(): lax.all_gather(w_xbc, ('dp', 'seq'), axis=0, tiled=True)  81.4 us
    unnamed x1, blocking collectives  34.8 us
    select_n x15, other arithmetic, hop(): jnp.where(position < mine, new, old)  24.3 us
    unnamed x51, local copies, waits for them, and re-layouts  23.3 us
    dot_general x1, matrix products, local(): jnp.dot(token_rows, lax.all_gather(w_xbc, ('dp', 'seq'), axis=0, tiled=Tr...  16.4 us
    dot_general x3, matrix products, block_inner(): jnp.einsum('hij,jhp->ihp', mixing, x_heads, precision=lax.Precision.HIGH)  16 us
    exp x15, local copies, waits for them, and re-layouts, combine_carry(): jnp.exp(later[0])[:, None, None] * earlier[1] + later[1]  10.4 us
  transfers between devices with their start and end apart: 3, of which 3 were waited for; matrix products, arithmetic and copies ran while one was open for 3% of the time, Pallas kernels for 0%

commit v1 on v0

--- a/solution.py
+++ b/solution.py
@@ -4,6 +4,14 @@
 from jax.sharding import PartitionSpec as P
 
 GROUP = 256
+
+
+def expand_the_spans(incoming_x, across):
+    copies = []
+    for _ in range(lax.axis_size(across)):
+        copies.append(incoming_x)
+    moved = jnp.concatenate(lax.all_to_all(jnp.stack(copies, axis=0), across, 0, 0), 0)
+    return moved
 
 
 def passed_along(value, axis, by):
@@ -67,9 +75,7 @@
     state_size = (channels - width_x) // 2
     kernel = conv_weight.shape[0]
     projected = jnp.dot(
-        token_rows,
-        lax.all_gather(w_xbc, ("dp", "seq"), axis=0, tiled=True),
-        preferred_element_type=jnp.float32,
+        token_rows, expand_the_spans(w_xbc, ("dp", "seq")), preferred_element_type=jnp.float32
     )
     xbc = projected.astype(jnp.bfloat16)
     rim_rows = passed_along(xbc[tok_count - (kernel - 1) :], "seq", 1)

time: 370 us -> 527 us (1.42)
  waiting for transfers between devices: 177 us -> 317 us
  starting transfers between devices: 3.15 us -> 13.8 us
    all_to_all x0 -> x1, waiting for transfers between devices: none -> 212 us  [expand_the_spans(): lax.all_to_all(jnp.stack(copies, axis=0), across, 0, 0)]
    all_gather x1 -> x0, waiting for transfers between devices: 81.4 us -> none  [local(): lax.all_gather(w_xbc, ('dp', 'seq'), axis=0, tiled=True)]
    unnamed x51 -> x58, local copies, waits for them, and re-layouts: 23.3 us -> 1.81 us
    reshape x1 -> x2, local copies, waits for them, and re-layouts: 0.01 us -> 20.5 us  [the longest x1 20.5 us: expand_the_spans(): jnp.concatenate(lax.all_to_all(jnp.stack(copies, axis=0), across, 0, 0), 0)]
    all_to_all x0 -> x1, starting transfers between devices: none -> 11.9 us  [expand_the_spans(): lax.all_to_all(jnp.stack(copies, axis=0), across, 0, 0)]
    all_gather x1, waiting for transfers between devices: 93.6 us -> 105 us  [prefix(): pieces = jax.tree.map(lambda part: lax.all_gather(part, axis), value)]
    another operation x6 -> x7, local copies, waits for them, and re-layouts: 0.34 us -> 7.39 us  [the longest x1 7.05 us: expand_the_spans(): jnp.stack(copies, axis=0)]
  transfers between devices with their start and end apart: 3 -> 3, of which waited for: 3 -> 3; matrix products, arithmetic and copies ran while one was open for 3% -> 2% of each run, Pallas kernels for 0% -> 0%
where the time goes in v1:
time: 527 us; the launch traced here: 525 us
  waiting for transfers between devices  317 us (60%)
  local copies, waits for them, and re-layouts  53.4 us (10%)
  matrix products  47.5 us (9%)
  other arithmetic  40.7 us (8%)
  blocking collectives  37 us (7%)
  between operations  14.6 us (3%)
  starting transfers between devices  13.8 us (3%)
    all_to_all x1, waiting for transfers between devices, expand_the_spans(): lax.all_to_all(jnp.stack(copies, axis=0), across, 0, 0)  212 us
    all_gather x1, waiting for transfers between devices, prefix(): pieces = jax.tree.map(lambda part: lax.all_gather(part, axis), value)  105 us
    unnamed x1, blocking collectives  37 us
    select_n x15, other arithmetic, hop(): jnp.where(position < mine, new, old)  24.3 us
    reshape x1, local copies, waits for them, and re-layouts, expand_the_spans(): jnp.concatenate(lax.all_to_all(jnp.stack(copies, axis=0), across, 0, 0), 0)  20.5 us
    dot_general x1, matrix products, local(): jnp.dot(token_rows, expand_the_spans(w_xbc, ('dp', 'seq')), preferred_ele...  16.4 us
    dot_general x3, matrix products, block_inner(): jnp.einsum('hij,jhp->ihp', mixing, x_heads, precision=lax.Precision.HIGH)  16 us
    all_to_all x1, starting transfers between devices, expand_the_spans(): lax.all_to_all(jnp.stack(copies, axis=0), across, 0, 0)  11.9 us
  transfers between devices with their start and end apart: 3, of which 3 were waited for; matrix products, arithmetic and copies ran while one was open for 2% of the time, Pallas kernels for 0%

profile of v1, /device:TPU:1, one launch (start us, length us, event | category | flops | bytes accessed | tf_op | source)
XLA Modules:
  0.0 524.8 jit_solution(882337907588553675)
XLA Ops:
  6.5 7.0 %stack.2 = bf16[128,20,2816]{2,1,0:T(8,128)(2,1)} broadcast(bf16[20,2816]{1,0:T(8,128)(2,1)} %param.11), dimensions={1,2} | broadcast | bytes 14530560 | tf_op jit(solution)/shard_map/stack | solution.py:13
  13.6 11.9 %all-to-all-start = ((bf16[128,20,2816]{2,1,0:T(8,128)(2,1)}), bf16[128,20,2816]{2,1,0:T(8,128)(2,1)}, u32[]{:S(2)}, u32[]{:S(2)}) async-start(bf16[128,20,2816]{2,1,0:T(8,128)(2,1)} %stack.2), calls=%async_computation | async-start | bytes 34603008 | tf_op jit(solution)/shard_map/all_to_all | solution.py:13
  29.2 0.8 fusion.91
  29.9 211.8 %all-to-all-done = bf16[128,20,2816]{2,1,0:T(8,128)(2,1)} async-done(((bf16[128,20,2816]{2,1,0:T(8,128)(2,1)}), bf16[128,20,2816]{2,1,0:T(8,128)(2,1)}, u32[]{:S(2)}, u32[]{:S(2)}) %all-to-all-start) | async-done | bytes 14417952 | tf_op jit(solution)/shard_map/all_to_all | solution.py:13
  241.7 20.5 %reshape.239 = bf16[2560,2816]{1,0:T(8,128)(2,1)} reshape(bf16[128,20,2816]{2,1,0:T(8,128)(2,1)} %all-to-all-done) | data formatting | bytes 28835840 | tf_op jit(solution)/shard_map/reshape | solution.py:13
  262.3 16.4 %convolution_convert_fusion = bf16[768,2816]{1,0:T(8,128)(2,1)S(1)} fusion(bf16[2560,2816]{1,0:T(8,128)(2,1)} %reshape.239, bf16[1,768,2560]{2,1,0:T(8,128)(2,1)} %param.10), kind=kOutput, calls=%fused_computation.42 | convolution fusion | flops 11075125248 | bytes 22675456 | tf_op jit(solution)/shard_map/dot_general | solution.py:77
  278.7 1.9 collective-permute-start
  280.8 0.7 collective-permute-done
  281.5 6.3 %multiply_convert_fusion = bf16[768,2816]{1,0:T(8,128)(2,1)S(1)} fusion(bf16[768,2816]{1,0:T(8,128)(2,1)S(1)} %convolution_convert_fusion, bf16[3,2816]{1,0:T(4,128)(2,1)S(1)} %collective-permute-done, f32[2816]{0:T(1024)S(1)} %get-tuple-element.120, f32[2816]{0:T(1024)S(1)} %get-tuple-element.121, f32[2816]{0:T(1024)S(1)} %get-tuple-element.119, ...), kind=kLoop, calls=%fused_computation.21 | loop fusion | flops 56229888 | bytes 8723968 | tf_op jit(solution)/shard_map/convert_element_type | solution.py:88
  287.8 2.0 fusion.90
  289.8 0.8 copy-done
  290.7 1.6 copy.33
  292.3 1.5 copy.41
  293.8 1.6 copy.40
  295.4 1.9 fusion.42
  297.3 1.8 fusion.40
  299.2 2.9 fusion.52
  303.5 37.0 %all-reduce = f32[640]{0:T(1024)S(1)} all-reduce(f32[640]{0:T(1024)S(1)} %dynamic-update-slice), channel_id=2, replica_groups=mesh['dp'=8,'seq'=16] {'seq'}, use_global_device_ids=true, to_apply=%add | all-reduce | flops 640 | bytes 5120
  341.9 1.1 fusion.83
  343.0 1.1 fusion.76
  344.1 1.1 fusion.73
  345.1 104.8 %all-gather.4.cloned.1.call-done = f32[640,64,128]{2,1,0:T(8,128)} async-done(((f32[40,64,128]{2,1,0:T(8,128)}), f32[640,64,128]{2,1,0:T(8,128)}) %all-gather.4.cloned.1.call-update) | async-done | bytes 20971536 | tf_op jit(solution)/shard_map/all_gather | solution.py:25
  449.9 35.1 %while.14 = (s32[]{:T(128)}, f32[40,64,128]{2,1,0:T(8,128)S(1)}, s32[]{:T(128)}, f32[16,40]{1,0:T(8,128)}, f32[16,40,64,128]{3,2,1,0:T(8,128)}, /*index=5*/s32[]{:T(128)}, s32[]{:T(128)}) while((s32[]{:T(128)}, f32[40,64,128]{2,1,0:T(8,128)S(1)}, s32[]{:T(128)}, f32[16,40]{1,0:T(8,128)}, f32[16,40,64,128]{3,2,1,0:T(8,128)}, ...), condition=%wide.region_7.8_spmd.clone, body=%wide.region_6.7_spmd.clone.sunk | while | flops 1310724 | bytes 3932753 | solution.py:34
  449.9 0.7 exponential_bitcast_fusion.5
  450.6 1.6 fusion.99
  452.2 0.7 exponential_bitcast_fusion.5
  452.9 1.6 fusion.99
  454.6 0.7 exponential_bitcast_fusion.5
  455.3 1.6 fusion.99
  456.9 0.7 exponential_bitcast_fusion.5
  457.6 1.6 fusion.99
  459.2 0.7 exponential_bitcast_fusion.5
  459.9 1.6 fusion.99
  461.6 0.7 exponential_bitcast_fusion.5
  462.2 1.6 fusion.99
  463.9 0.7 exponential_bitcast_fusion.5
  464.6 1.6 fusion.99
  466.2 0.7 exponential_bitcast_fusion.5
  466.9 1.6 fusion.99
  468.5 0.7 exponential_bitcast_fusion.5
  469.2 1.6 fusion.99
  470.9 0.7 exponential_bitcast_fusion.5
  471.6 1.6 fusion.99
  473.2 0.7 exponential_bitcast_fusion.5
  473.9 1.6 fusion.99
  475.5 0.7 exponential_bitcast_fusion.5
  476.2 1.6 fusion.99
  477.9 0.7 exponential_bitcast_fusion.5
  478.5 1.6 fusion.99
  480.2 0.7 exponential_bitcast_fusion.5
  480.9 1.6 fusion.99
  482.5 0.7 exponential_bitcast_fusion.5
  483.2 1.6 fusion.99
  485.0 1.7 fusion.70
  486.8 1.8 fusion.60
  488.7 1.8 fusion.53
  490.6 5.3 %multiply_reduce_fusion.2 = (f32[256,40]{0,1:T(8,128)S(1)}, f32[256,40,64]{0,2,1:T(8,128)S(1)}) fusion(bf16[256,40,64]{0,2,1:T(8,128)(2,1)S(1)} %bitcast.137, f32[40]{0:T(128)S(1)} %copy-done.25, f32[256,40,64]{0,2,1:T(8,128)S(1)} %fusion.70, f32[256,40]{0,1:T(8,128)S(1)} %copy-done.18, f32[40,256]{1,0:T(8,128)S(1)} %copy-done.17, ...), kind=kOutput, calls=%fused_computation.68 | convolution fusion | flops 1021696000 | bytes 7045280 | tf_op jit(solution)/shard_map/hij,jhp->ihp/dot_general | solution.py:60
  496.0 5.5 %multiply_reduce_fusion.1 = (f32[256,40]{0,1:T(8,128)S(1)}, f32[256,40,64]{0,2,1:T(8,128)S(1)}) fusion(bf16[256,40,64]{0,2,1:T(8,128)(2,1)S(1)} %bitcast.135, f32[40]{0:T(128)S(1)} %copy-done.25, f32[256,40,64]{0,2,1:T(8,128)S(1)} %fusion.60, f32[256,40]{0,1:T(8,128)S(1)} %copy-done.16, f32[40,256]{1,0:T(8,128)S(1)} %copy-done.15, ...), kind=kOutput, calls=%fused_computation.66 | convolution fusion | flops 1021696000 | bytes 7045280 | tf_op jit(solution)/shard_map/hij,jhp->ihp/dot_general | solution.py:60
  501.5 5.2 %multiply_reduce_fusion = (f32[256,40]{0,1:T(8,128)S(1)}, f32[256,40,64]{0,2,1:T(8,128)S(1)}) fusion(bf16[256,40,64]{0,2,1:T(8,128)(2,1)S(1)} %bitcast.139, f32[40]{0:T(128)S(1)} %copy-done.25, f32[256,40,64]{0,2,1:T(8,128)S(1)} %fusion.53, f32[256,40]{0,1:T(8,128)S(1)} %copy-done.14, f32[40,256]{1,0:T(8,128)S(1)} %copy-done.13, ...), kind=kOutput, calls=%fused_computation.64 | convolution fusion | flops 1021696000 | bytes 7045280 | tf_op jit(solution)/shard_map/hij,jhp->ihp/dot_general | solution.py:60
  506.8 2.2 multiply_convert_fusion.3
  509.0 2.4 copy.44
  511.5 1.6 copy.43
  513.1 1.6 copy.42
  514.6 3.3 maximum_bitcast_fusion
  (91 shorter events, 6.2 us)
Async XLA Ops:
  13.6 11.9 %copy-start.24 = (f32[40]{0:T(128)S(1)}, f32[40]{0:T(128)}, u32[]{:S(2)}) copy-start(f32[40]{0:T(128)} %param.14) | copy-start | bytes 484
  13.6 12.0 %copy-start.10 = (f32[1,40,768]{2,1,0:T(8,128)S(1)}, f32[1,40,768]{2,1,0:T(8,128)}, u32[]{:S(2)}) copy-start(f32[1,40,768]{2,1,0:T(8,128)} %param.15) | copy-start | bytes 368644
  13.6 228.2 %all-to-all-start = ((bf16[128,20,2816]{2,1,0:T(8,128)(2,1)}), bf16[128,20,2816]{2,1,0:T(8,128)(2,1)}, u32[]{:S(2)}, u32[]{:S(2)}) async-start(bf16[128,20,2816]{2,1,0:T(8,128)(2,1)} %stack.2), calls=%async_computation | async-start | bytes 34603008 | tf_op jit(solution)/shard_map/all_to_all | solution.py:13
  25.5 424.4 %all-gather.4.cloned.1.call-start = ((), (), s32[]{:S(2)}) async-start(), calls=%async_computation.1 | async-start | bytes 22282240 | tf_op jit(solution)/shard_map/all_gather | solution.py:25
  262.2 18.4 %copy-start.12 = (f32[4,2816]{1,0:T(4,128)S(1)}, f32[4,2816]{1,0:T(4,128)}, u32[]{:S(2)}) copy-start(f32[4,2816]{1,0:T(4,128)} %param.12) | copy-start | bytes 135172
  262.2 19.3 %copy-start.19 = (f32[2816]{0:T(1024)S(1)}, f32[2816]{0:T(1024)}, u32[]{:S(2)}) copy-start(f32[2816]{0:T(1024)} %param.13) | copy-start | bytes 33796
  278.7 2.8 collective-permute-start
  280.7 18.4 %copy-start.22 = (f32[40]{0:T(128)}, f32[40]{0:T(128)S(1)}, u32[]{:S(2)}) copy-start(f32[40]{0:T(128)S(1)} %exp.81) | copy-start | bytes 484
  287.8 2.8 copy-start
  292.3 5.1 copy-start.5
  295.4 1.9 copy-start.3
  295.4 3.7 copy-start.7
  297.3 1.8 copy-start.1
  299.2 2.9 copy-start.26
  299.2 42.1 %copy-start.20 = (f32[2560]{0:T(1024)S(1)}, f32[2560]{0:T(1024)}, u32[]{:S(2)}) copy-start(f32[2560]{0:T(1024)} %param.17) | copy-start | bytes 30724
  485.0 1.7 copy-start.21
  486.7 1.9 copy-start.2
  486.7 1.9 copy-start.23
  488.6 1.9 copy-start.6
  488.6 1.9 copy-start.11
  488.6 1.9 copy-start.17
  488.6 1.9 copy-start.18
  488.7 1.9 copy-start.25
  490.6 5.3 %copy-start.4 = (bf16[256,2560]{0,1:T(8,128)(2,1)S(1)}, bf16[256,2560]{0,1:T(8,128)(2,1)}, u32[]{:S(2)}) copy-start(bf16[256,2560]{0,1:T(8,128)(2,1)} %copy-done.3) | copy-start | bytes 3932164
  490.6 5.3 %copy-start.15 = (f32[40,256]{1,0:T(8,128)S(1)}, f32[40,256]{1,0:T(8,128)}, u32[]{:S(2)}) copy-start(f32[40,256]{1,0:T(8,128)} %get-tuple-element.143) | copy-start | bytes 122884
  490.6 5.3 %copy-start.16 = (f32[256,40]{0,1:T(8,128)S(1)}, f32[256,40]{0,1:T(8,128)}, u32[]{:S(2)}) copy-start(f32[256,40]{0,1:T(8,128)} %get-tuple-element.152) | copy-start | bytes 122884
  495.9 5.6 %copy-start.8 = (bf16[256,2560]{0,1:T(8,128)(2,1)S(1)}, bf16[256,2560]{0,1:T(8,128)(2,1)}, u32[]{:S(2)}) copy-start(bf16[256,2560]{0,1:T(8,128)(2,1)} %copy.41) | copy-start | bytes 3932164
  495.9 5.6 %copy-start.13 = (f32[40,256]{1,0:T(8,128)S(1)}, f32[40,256]{1,0:T(8,128)}, u32[]{:S(2)}) copy-start(f32[40,256]{1,0:T(8,128)} %get-tuple-element.142) | copy-start | bytes 122884
  496.0 5.6 %copy-start.14 = (f32[256,40]{0,1:T(8,128)S(1)}, f32[256,40]{0,1:T(8,128)}, u32[]{:S(2)}) copy-start(f32[256,40]{0,1:T(8,128)} %get-tuple-element.151) | copy-start | bytes 122884
  513.1 1.6 copy-start.9
Sparse Core Ops, SparseCore 0:
  302.2 147.6 all-gather.3
